TPU v7x, 128 devices: a whole 4x4x4 slice. The times are simulated.
128 devices in a mesh: seq: 16 (over x_lo, z, core), tp: 8 (over y, x_hi).
Axes of the slice: x: 4 (x_hi: 2, x_lo: 2; x = x_hi * 2 + x_lo), y: 4, z: 4, core: 2. Of those that a mesh axis runs over, the one named last changes fastest.
Arguments:
- hidden_in: bfloat16 [6144, 3584], P('seq'), may hold values from -48 to 48
- joined_inputs: bfloat16 [6144, 8192], P('seq', 'tp'), may hold values from -64 to 64
- lengths: int32 [4], replicated, may hold values from 1 to 3072, 6144 in all
- o_weight: bfloat16 [4096, 3584], P('tp'), may hold values from -0.09375 to 0.09375
- gate_up: float32 [2, 3584, 7168], P(None, ('seq', 'tp')), may hold values from -0.09375 to 0.09375
- down_weight: bfloat16 [7168, 3584], P('tp'), may hold values from -0.0625 to 0.0625
- next_weight: bfloat16 [3584, 8192], P(None, 'tp'), may hold values from -0.09375 to 0.09375
- post_attn_gain: float32 [3584], replicated, may hold values from 0.1 to 1.9
- pre_ffw_gain: float32 [3584], replicated, may hold values from 0.1 to 1.9
- post_ffw_gain: float32 [3584], replicated, may hold values from 0.1 to 1.9
- next_gain: float32 [3584], replicated, may hold values from 0.1 to 1.9
Outputs:
- next_qkv: bfloat16 [6144, 8192], P('seq', 'tp')
Inputs may be any that keep to these rules, and one draw needn't show every extreme that they name: The lengths of 4 prompts laid end to end; they sum to 6144 and the longest is exactly 3072.
All inputs are finite; a program needn't handle non-finite values.
Results may differ from a plain program's by a relative error of at most 0.022.
Values may be sent and summed in bfloat16 or wider, within the bound.
A program may use at most 192 MiB of HBM per device.

v0:
```python
import jax
import jax.numpy as jnp
from jax import lax
from jax.sharding import PartitionSpec as P

HEADS = 16
KV_HEADS = 8
HEAD_DIM = 256


def rms_norm(values, gain):
    meansq = jnp.mean(values * values, axis=-1, keepdims=True)
    return values * lax.rsqrt(meansq + 1e-06) * gain


def local(
    hidden_in,
    joined_inputs,
    lengths,
    o_weight,
    gate_up,
    down_weight,
    next_weight,
    post_attn_gain,
    pre_ffw_gain,
    post_ffw_gain,
    next_gain,
):
    seq_count = lax.axis_size("seq")
    tp_count = lax.axis_size("tp")
    row_count = hidden_in.shape[0]
    model_width = hidden_in.shape[1]
    per_group = HEADS // KV_HEADS
    group_cols = (per_group + 2) * HEAD_DIM
    local_groups = joined_inputs.shape[1] // group_cols
    grouped = joined_inputs.reshape(row_count, local_groups, group_cols)
    queries = grouped[:, :, : per_group * HEAD_DIM].reshape(
        row_count, local_groups, per_group, HEAD_DIM
    )
    own_keys = grouped[:, :, per_group * HEAD_DIM : (per_group + 1) * HEAD_DIM]
    own_values = grouped[:, :, (per_group + 1) * HEAD_DIM :]
    keys_all, values_all = (
        lax.all_gather(own_keys, "seq", axis=0, tiled=True),
        lax.all_gather(own_values, "seq", axis=0, tiled=True),
    )
    total_rows = keys_all.shape[0]
    seq_index = lax.axis_index("seq")
    position = seq_index * row_count
    ends = jnp.cumsum(lengths)
    places = jnp.arange(total_rows, dtype=jnp.int32)
    prompt_ids = jnp.sum((places[:, None] >= ends[None, :]).astype(jnp.int32), axis=1)
    query_place = position + jnp.arange(row_count, dtype=jnp.int32)
    query_ids = lax.dynamic_slice_in_dim(prompt_ids, position, row_count, 0)
    scale = HEAD_DIM ** (-0.5)
    scores = (
        jnp.einsum("qgrd,kgd->qgrk", queries, keys_all, preferred_element_type=jnp.float32) * scale
    )
    allowed = (
        (query_ids[:, None] == prompt_ids[None, :]) & (places[None, :] <= query_place[:, None])
    )[:, None, None, :]
    scores = jnp.where(allowed, scores, -jnp.inf)
    peak = jnp.max(scores, axis=-1, keepdims=True)
    weights = jnp.where(allowed, jnp.exp(scores - peak), 0.0)
    norm_sum = jnp.sum(weights, axis=-1)
    blended = jnp.einsum(
        "qgrk,kgd->qgrd",
        weights.astype(jnp.bfloat16),
        values_all,
        preferred_element_type=jnp.float32,
    )
    blended = blended / norm_sum[..., None]
    attended = blended.astype(jnp.bfloat16).reshape(row_count, local_groups * per_group * HEAD_DIM)
    projected = jnp.dot(attended, o_weight, preferred_element_type=jnp.float32)

    def total_of(values):
        return lax.psum(values.astype(jnp.bfloat16), "tp").astype(jnp.float32)

    residual_mid = hidden_in.astype(jnp.float32) + rms_norm(total_of(projected), post_attn_gain)
    ffw_in = rms_norm(residual_mid, pre_ffw_gain).astype(jnp.bfloat16)
    server_low = gate_up.astype(jnp.bfloat16)
    stacked_rows = lax.all_gather(server_low, "seq", axis=1, tiled=True)
    local_units = lax.all_to_all(stacked_rows, "tp", split_axis=2, concat_axis=1, tiled=True)
    piece_rows = gate_up.shape[1]
    reordered = (
        ffw_in.reshape(row_count, seq_count, tp_count, piece_rows)
        .transpose(0, 2, 1, 3)
        .reshape(row_count, model_width)
    )
    gate = jnp.dot(reordered, local_units[0], preferred_element_type=jnp.float32)
    up_part = jnp.dot(reordered, local_units[1], preferred_element_type=jnp.float32)
    activated = (jax.nn.gelu(gate, approximate=True) * up_part).astype(jnp.bfloat16)
    ffw_out = jnp.dot(activated, down_weight, preferred_element_type=jnp.float32)
    residual_out = residual_mid + rms_norm(total_of(ffw_out), post_ffw_gain)
    next_in = rms_norm(residual_out, next_gain).astype(jnp.bfloat16)
    return jnp.dot(next_in, next_weight, preferred_element_type=jnp.float32).astype(jnp.bfloat16)


def solution(mesh):
    in_specs = (
        P("seq", None),
        P("seq", "tp"),
        P(),
        P("tp", None),
        P(None, ("seq", "tp"), None),
        P("tp", None),
        P(None, "tp"),
        P(),
        P(),
        P(),
        P(),
    )
    out_specs = P("seq", "tp")
    return jax.shard_map(local, mesh=mesh, in_specs=in_specs, out_specs=out_specs, check_vma=False)
```

profile of v0, /device:TPU:1, one launch (start us, length us, event | category | flops | bytes accessed | tf_op | source)
XLA Modules:
  0.0 658.8 jit_solution(18442453555862474000)
XLA Ops:
  6.5 0.0 all-gather.8.cloned.1.call-start
  6.5 2.9 convert_element_type.50
  9.4 0.0 all-gather.8.cloned.1.call-update
  9.4 0.0 all-gather.4.cloned.1.call-start
  9.5 1.8 fusion.53
  11.3 0.0 all-gather.4.cloned.1.call-update
  11.3 0.0 all-gather.6.cloned.1.call-start
  11.4 0.7 all-gather.6.cloned.1.call-update
  12.1 1.0 slice.23
  13.1 0.8 reduce-window.8
  13.9 0.2 copy.49
  14.1 0.1 convert_reduce_fusion
  14.3 0.1 dynamic_slice.3
  14.4 72.0 %all-gather.8.cloned.1.call-done = bf16[2,448,7168]{2,0,1:T(2,128)(2,1)} async-done(((bf16[2,28,7168]{2,0,1:T(2,128)(2,1)}), bf16[2,448,7168]{2,0,1:T(2,128)(2,1)}) %all-gather.8.cloned.1.call-update) | async-done | bytes 12845072 | tf_op jit(solution)/shard_map/all_gather | solution.py:81
  86.4 48.5 %copy.55 = bf16[2,448,7168]{1,0,2:T(2,128)(2,1)} copy(bf16[2,448,7168]{2,0,1:T(2,128)(2,1)} %all-gather.8.cloned.1.call-done) | data formatting | bytes 25690112 | tf_op jit(solution)/shard_map/all_gather | solution.py:81
  134.9 6.5 all-to-all-start
  141.4 0.0 all-reduce.3.cloned.1.call-start
  141.5 3.8 fusion.6
  145.2 5.4 fusion
  150.7 6.5 copy-done.2
  157.2 6.1 fusion.1
  163.3 4.7 all-gather.6.cloned.1.call-done
  167.9 13.2 %fusion.39 = bf16[1,256,384,2]{2,1,3,0:T(8,128)(2,1)S(1)} fusion(bf16[6144,1,256]{2,0,1:T(8,128)(2,1)} %all-gather.6.cloned.1.call-done, f32[6144,384,2]{1,0,2:T(8,128)} %copy-done.2, f32[384,2]{0,1:T(2,128)S(1)} %get-tuple-element.9, pred[384,6144]{0,1:T(8,128)(4,1)} %fusion.6, f32[384,2]{0,1:T(2,128)S(1)} %fusion.1), kind=kOutput, calls=%fused_computation.45 | convolution fusion | flops 2439905280 | bytes 24778752 | tf_op jit(solution)/shard_map/qgrk,kgd->qgrd/dot_general | solution.py:65
  181.1 0.0 copy-start.5
  181.2 3.2 convolution_convert_fusion
  184.3 0.0 all-reduce.3.cloned.1.call-update
  184.4 0.2 all-reduce.5.cloned.1.call-start
  184.6 232.3 %all-reduce.3.cloned.1.call-done = bf16[384,3584]{1,0:T(8,128)(2,1)} async-done(((bf16[384,3584]{1,0:T(8,128)(2,1)}), bf16[384,3584]{1,0:T(8,128)(2,1)}) %all-reduce.3.cloned.1.call-update) | async-done | bytes 2752528 | tf_op jit(solution)/shard_map/psum | solution.py:76
  416.9 2.5 fusion.8
  419.5 4.0 multiply_reduce_fusion.1
  423.5 5.1 multiply_convert_fusion.1
  428.7 4.5 copy.53
  433.2 5.2 reshape.159
  438.4 4.0 copy.54
  442.4 5.2 reshape.160
  447.6 0.0 all-to-all-done
  447.6 24.5 %copy.63 = bf16[2,448,8,896]{3,2,1,0:T(8,128)(2,1)} copy(bf16[2,448,8,896]{1,0,3,2:T(2,128)(2,1)} %bitcast.16) | data formatting | bytes 25690112 | tf_op jit(solution)/shard_map/all_to_all | solution.py:82
  472.1 8.3 %fusion.52 = (bf16[1,8,448,896]{3,1,2,0:T(8,128)(2,1)}, bf16[1,8,448,896]{3,1,2,0:T(8,128)(2,1)S(1)}) fusion(bf16[2,8,448,896]{3,1,2,0:T(8,128)(2,1)} %bitcast.80), kind=kLoop, calls=%fused_computation.60 | loop fusion | bytes 25690112 | tf_op jit(solution)/shard_map/slice | solution.py:89
  480.4 3.9 copy.57
  484.3 3.8 copy.58
  488.1 5.9 fusion.54
  494.0 13.5 %convolution_convert_fusion.1 = bf16[384,3584]{1,0:T(8,128)(2,1)} fusion(bf16[896,3584]{1,0:T(8,128)(2,1)} %param.16, bf16[384,3584]{0,1:T(8,128)(2,1)} %reshape.160, bf16[3584,896]{1,0:T(8,128)(2,1)} %bitcast.83, f32[384,896]{1,0:T(8,128)} %fusion.54), kind=kOutput, calls=%fused_computation.15 | convolution fusion | flops 4937318400 | bytes 19726336 | tf_op jit(solution)/shard_map/dot_general | solution.py:92
  507.4 0.0 all-reduce.5.cloned.1.call-update
  507.5 0.0 copy-start.8
  507.5 129.4 %all-reduce.5.cloned.1.call-done = bf16[384,3584]{1,0:T(8,128)(2,1)} async-done(((bf16[384,3584]{1,0:T(8,128)(2,1)}), bf16[384,3584]{1,0:T(8,128)(2,1)}) %all-reduce.5.cloned.1.call-update) | async-done | bytes 2752528 | tf_op jit(solution)/shard_map/psum | solution.py:76
  636.9 2.5 fusion.11
  639.5 4.8 multiply_reduce_fusion
  644.3 8.0 %fusion.20 = bf16[384,1024]{1,0:T(8,128)(2,1)} fusion(bf16[3584,1024]{1,0:T(8,128)(2,1)} %param.17, f32[3584]{0:T(1024)S(1)} %copy-done.8, f32[384]{0:T(512)S(1)} %add_rsqrt_fusion, bf16[384,3584]{1,0:T(8,128)(2,1)S(1)} %copy-done.3, bf16[384,3584]{1,0:T(8,128)(2,1)S(1)} %copy-done, bf16[384,3584]{1,0:T(8,128)(2,1)S(1)} %copy-done.1, ...), kind=kOutput, calls=%fused_computation.34 | convolution fusion | flops 2835480576 | bytes 16431616 | tf_op jit(solution)/shard_map/dot_general | solution.py:95
  (21 shorter events, 0.1 us)
Async XLA Ops:
  6.5 79.8 %all-gather.8.cloned.1.call-start = ((), (), s32[]{:S(2)}) async-start(), calls=%async_computation.4 | async-start | bytes 13647872 | tf_op jit(solution)/shard_map/all_gather | solution.py:81
  9.4 135.8 %all-gather.4.cloned.1.call-start = ((), (), s32[]{:S(2)}) async-start(), calls=%async_computation.1 | async-start | bytes 3342336 | tf_op jit(solution)/shard_map/all_gather | solution.py:43
  11.3 156.6 %all-gather.6.cloned.1.call-start = ((), (), s32[]{:S(2)}) async-start(), calls=%async_computation.2 | async-start | bytes 3342336 | tf_op jit(solution)/shard_map/all_gather | solution.py:44
  134.9 312.7 %all-to-all-start = ((bf16[2,448,7168]{1,0,2:T(2,128)(2,1)}), bf16[2,448,7168]{1,0,2:T(2,128)(2,1)}, u32[]{:S(2)}, u32[]{:S(2)}) async-start(bf16[2,448,7168]{1,0,2:T(2,128)(2,1)} %copy.55), calls=%async_computation | async-start | bytes 29360128 | tf_op jit(solution)/shard_map/all_to_all | solution.py:82
  141.4 275.5 %all-reduce.3.cloned.1.call-start = ((), (), s32[]{:S(2)}) async-start(), calls=%async_computation.3 | async-start | bytes 5505024 | tf_op jit(solution)/shard_map/psum | solution.py:76
  150.7 6.5 copy-start.2
  167.9 13.2 %copy-start.4 = (bf16[512,3584]{1,0:T(8,128)(2,1)S(1)}, bf16[512,3584]{1,0:T(8,128)(2,1)}, u32[]{:S(2)}) copy-start(bf16[512,3584]{1,0:T(8,128)(2,1)} %param.14) | copy-start | bytes 11010052
  181.1 238.4 %copy-start.5 = (f32[3584]{0:T(1024)S(1)}, f32[3584]{0:T(1024)}, u32[]{:S(2)}) copy-start(f32[3584]{0:T(1024)} %param.18) | copy-start | bytes 43012
  184.3 239.2 %copy-start.6 = (f32[3584]{0:T(1024)S(1)}, f32[3584]{0:T(1024)}, u32[]{:S(2)}) copy-start(f32[3584]{0:T(1024)} %param.19) | copy-start | bytes 43012
  184.4 452.5 %all-reduce.5.cloned.1.call-start = ((), (), s32[]{:S(2)}) async-start(), calls=%async_computation.5 | async-start | bytes 5505024 | tf_op jit(solution)/shard_map/psum | solution.py:76
  416.9 6.6 copy-start
  507.4 132.0 %copy-start.7 = (f32[3584]{0:T(1024)S(1)}, f32[3584]{0:T(1024)}, u32[]{:S(2)}) copy-start(f32[3584]{0:T(1024)} %param.20) | copy-start | bytes 43012
  507.5 136.8 %copy-start.8 = (f32[3584]{0:T(1024)S(1)}, f32[3584]{0:T(1024)}, u32[]{:S(2)}) copy-start(f32[3584]{0:T(1024)} %param.21) | copy-start | bytes 43012
  636.9 7.4 %copy-start.1 = (bf16[384,3584]{1,0:T(8,128)(2,1)S(1)}, bf16[384,3584]{1,0:T(8,128)(2,1)}, u32[]{:S(2)}) copy-start(bf16[384,3584]{1,0:T(8,128)(2,1)} %param.11) | copy-start | bytes 8257540
  636.9 7.4 %copy-start.3 = (bf16[384,3584]{1,0:T(8,128)(2,1)S(1)}, bf16[384,3584]{1,0:T(8,128)(2,1)}, u32[]{:S(2)}) copy-start(bf16[384,3584]{1,0:T(8,128)(2,1)} %all-reduce.5.cloned.1.call-done) | copy-start | bytes 8257540
Sparse Core Ops, SparseCore 0:
  9.6 76.7 all-gather.7
  88.1 37.0 all-gather.3
  126.8 41.0 all-gather.5
  184.5 232.4 all-reduce.2
  507.6 129.2 all-reduce.4
where the time goes:
time: 662 us; the launch traced here: 659 us
  waiting for transfers between devices  439 us (66%)
  local copies, waits for them, and re-layouts  118 us (18%)
  matrix products  49.1 us (7%)
  other arithmetic  32.8 us (5%)
  between operations  13.3 us (2%)
  starting transfers between devices  6.85 us (1%)
    psum x2, waiting for transfers between devices, total_of(): return lax.psum(values.astype(jnp.bfloat16), 'tp').astype(jnp.float32)  362 us
    all_gather x1, waiting for transfers between devices, local(): stacked_rows = lax.all_gather(server_low, 'seq', axis=1, tiled=True)  72 us
    all_gather x1, local copies, waits for them, and re-layouts, local(): stacked_rows = lax.all_gather(server_low, 'seq', axis=1, tiled=True)  48.5 us
    all_to_all x1, local copies, waits for them, and re-layouts, local(): lax.all_to_all(stacked_rows, 'tp', split_axis=2, concat_axis=1, tiled=True)  24.5 us
    reduce_sum x4, other arithmetic, rms_norm(): meansq = jnp.mean(values * values, axis=-1, keepdims=True)  13.9 us
    dot_general x1, matrix products, local(): jnp.dot(activated, down_weight, preferred_element_type=jnp.float32)  13.5 us
  transfers between devices with their start and end apart: 6, of which 4 were waited for; matrix products, arithmetic and copies ran while one was open for 17% of the time, Pallas kernels for 0%

commit v1 on v0

--- a/solution.py
+++ b/solution.py
@@ -79,7 +79,10 @@
     ffw_in = rms_norm(residual_mid, pre_ffw_gain).astype(jnp.bfloat16)
     server_low = gate_up.astype(jnp.bfloat16)
     stacked_rows = lax.all_gather(server_low, "seq", axis=1, tiled=True)
-    local_units = lax.all_to_all(stacked_rows, "tp", split_axis=2, concat_axis=1, tiled=True)
+    local_units = jnp.concatenate(
+        lax.all_to_all(jnp.stack(jnp.split(stacked_rows, lax.axis_size("tp"), axis=2)), "tp", 0, 0),
+        axis=1,
+    )
     piece_rows = gate_up.shape[1]
     reordered = (
         ffw_in.reshape(row_count, seq_count, tp_count, piece_rows)

time: 662 us -> 601 us (0.908); the launches traced: 659 us -> 591 us
  local copies, waits for them, and re-layouts: 118 us -> 65.9 us
  waiting for transfers between devices: 439 us -> 414 us
  starting transfers between devices: 6.85 us -> 17.1 us
    all_gather x1 -> x0, local copies, waits for them, and re-layouts: 48.5 us -> none  [local(): stacked_rows = lax.all_gather(server_low, 'seq', axis=1, tiled=True)]
    psum x2, waiting for transfers between devices: 362 us -> 325 us  [total_of(): return lax.psum(values.astype(jnp.bfloat16), 'tp').astype(jnp.float32)]
    unnamed x18 -> x27, local copies, waits for them, and re-layouts: 6.5 us -> 25.2 us
    all_to_all x1, local copies, waits for them, and re-layouts: 24.5 us -> 6.7 us  [local(): lax.all_to_all(jnp.stack(jnp.split(stacked_rows, lax.axis_size('tp'), axi...]
    all_gather x1, waiting for transfers between devices: 4.66 us -> 16.6 us  [local(): lax.all_gather(own_values, 'seq', axis=0, tiled=True)]
    psum x2, starting transfers between devices: 0.26 us -> 10.6 us  [total_of(): return lax.psum(values.astype(jnp.bfloat16), 'tp').astype(jnp.float32)]
    slice x2 -> x1, local copies, waits for them, and re-layouts: 12.2 us -> 3.42 us  [local(): local_units[0]]
    another operation x0 -> x2, local copies, waits for them, and re-layouts: none -> 8.46 us  [local(): jnp.stack(jnp.split(stacked_rows, lax.axis_size('tp'), axis=2))]
  transfers between devices with their start and end apart: 6 -> 6, of which waited for: 4 -> 4; matrix products, arithmetic and copies ran while one was open for 17% -> 16% of each run, Pallas kernels for 0% -> 0%
where the time goes in v1:
time: 601 us; the launch traced here: 591 us
  waiting for transfers between devices  414 us (69%)
  local copies, waits for them, and re-layouts  65.9 us (11%)
  matrix products  47.2 us (8%)
  other arithmetic  32.9 us (5%)
  starting transfers between devices  17.1 us (3%)
  between operations  13.7 us (2%)
    psum x2, waiting for transfers between devices, total_of(): return lax.psum(values.astype(jnp.bfloat16), 'tp').astype(jnp.float32)  325 us
    all_gather x1, waiting for transfers between devices, local(): stacked_rows = lax.all_gather(server_low, 'seq', axis=1, tiled=True)  72 us
    unnamed x27, local copies, waits for them, and re-layouts  25.2 us
    all_gather x1, waiting for transfers between devices, local(): lax.all_gather(own_values, 'seq', axis=0, tiled=True)  16.6 us
    reduce_sum x4, other arithmetic, rms_norm(): meansq = jnp.mean(values * values, axis=-1, keepdims=True)  13.9 us
    dot_general x1, matrix products, local(): jnp.dot(activated, down_weight, preferred_element_type=jnp.float32)  13.4 us
    dot_general x1, matrix products, local(): jnp.einsum('qgrk,kgd->qgrd', weights.astype(jnp.bfloat16), values_all, pr...  13.2 us
  transfers between devices with their start and end apart: 6, of which 4 were waited for; matrix products, arithmetic and copies ran while one was open for 16% of the time, Pallas kernels for 0%

profile of v1, /device:TPU:1, one launch (start us, length us, event | category | flops | bytes accessed | tf_op | source)
XLA Modules:
  0.0 591.1 jit_solution(2048562144768185990)
XLA Ops:
  6.5 2.9 convert_element_type.50
  9.4 0.0 all-gather.4.cloned.1.call-start
  9.5 1.8 fusion.61
  11.3 0.0 all-gather.4.cloned.1.call-update
  11.3 0.0 all-gather.6.cloned.1.call-start
  11.4 0.7 all-gather.6.cloned.1.call-update
  12.1 1.0 slice.23
  13.1 0.8 reduce-window.8
  13.9 0.1 convert_reduce_fusion
  14.1 0.2 copy.36
  14.3 0.1 dynamic_slice.3
  14.4 72.0 %all-gather.8.cloned.1.call-done = bf16[2,448,7168]{2,0,1:T(2,128)(2,1)} async-done(((bf16[2,28,7168]{2,0,1:T(2,128)(2,1)}), bf16[2,448,7168]{2,0,1:T(2,128)(2,1)}) %all-gather.8.cloned.1.call-update) | async-done | bytes 12845072 | tf_op jit(solution)/shard_map/all_gather | solution.py:81
  86.4 2.5 fusion.27
  88.9 2.7 fusion.26
  91.6 2.7 fusion.25
  94.3 2.7 fusion.24
  96.9 2.8 fusion.23
  99.7 2.7 fusion.22
  102.4 2.7 fusion.21
  105.1 2.7 fusion.20
  107.8 5.8 copy.42
  113.6 6.3 %all-to-all-start = ((bf16[8,2,448,896]{3,2,1,0:T(8,128)(2,1)}), bf16[8,2,448,896]{3,2,1,0:T(8,128)(2,1)}, u32[]{:S(2)}, u32[]{:S(2)}) async-start(bf16[8,2,448,896]{3,2,1,0:T(8,128)(2,1)} %copy.42), calls=%async_computation | async-start | bytes 25690112 | tf_op jit(solution)/shard_map/all_to_all | solution.py:83
  119.9 10.6 %all-reduce.3.cloned.1.call-start = ((), (), s32[]{:S(2)}) async-start(), calls=%async_computation.3 | async-start | bytes 5505024 | tf_op jit(solution)/shard_map/psum | solution.py:76
  130.5 3.8 fusion.6
  134.4 5.4 fusion
  139.8 6.5 %copy-done.3 = f32[6144,384,2]{1,0,2:T(8,128)} copy-done((f32[6144,384,2]{1,0,2:T(8,128)}, f32[6144,384,2]{1,0,2:T(8,128)S(1)}, u32[]{:S(2)}) %copy-start.3) | copy-done | bytes 18874392
  146.3 6.1 %fusion.1 = f32[384,2]{0,1:T(2,128)S(1)} fusion(f32[6144,384,2]{1,0,2:T(8,128)S(1)} %get-tuple-element.10, f32[384,2]{0,1:T(2,128)S(1)} %get-tuple-element.9, pred[384,6144]{0,1:T(8,128)(4,1)} %fusion.6), kind=kLoop, calls=%fused_computation.3 | loop fusion | flops 23592192 | bytes 21239808 | tf_op jit(solution)/shard_map/reduce_sum | solution.py:64
  152.4 16.6 %all-gather.6.cloned.1.call-done = bf16[6144,1,256]{2,0,1:T(8,128)(2,1)} async-done(((bf16[384,1,256]{2,0,1:T(8,128)(2,1)}), bf16[6144,1,256]{2,0,1:T(8,128)(2,1)}) %all-gather.6.cloned.1.call-update) | async-done | bytes 3145744 | tf_op jit(solution)/shard_map/all_gather | solution.py:44
  169.0 13.2 %fusion.47 = bf16[1,256,384,2]{2,1,3,0:T(8,128)(2,1)S(1)} fusion(bf16[6144,1,256]{2,0,1:T(8,128)(2,1)} %all-gather.6.cloned.1.call-done, f32[6144,384,2]{1,0,2:T(8,128)} %copy-done.3, f32[384,2]{0,1:T(2,128)S(1)} %get-tuple-element.9, pred[384,6144]{0,1:T(8,128)(4,1)} %fusion.6, f32[384,2]{0,1:T(2,128)S(1)} %fusion.1), kind=kOutput, calls=%fused_computation.62 | convolution fusion | flops 2439905280 | bytes 24778752 | tf_op jit(solution)/shard_map/qgrk,kgd->qgrd/dot_general | solution.py:65
  182.2 3.2 convolution_convert_fusion
  185.4 0.0 all-reduce.3.cloned.1.call-update
  185.4 0.0 all-reduce.5.cloned.1.call-start
  185.5 196.7 %all-reduce.3.cloned.1.call-done = bf16[384,3584]{1,0:T(8,128)(2,1)} async-done(((bf16[384,3584]{1,0:T(8,128)(2,1)}), bf16[384,3584]{1,0:T(8,128)(2,1)}) %all-reduce.3.cloned.1.call-update) | async-done | bytes 2752528 | tf_op jit(solution)/shard_map/psum | solution.py:76
  382.2 2.5 fusion.8
  384.7 4.0 multiply_reduce_fusion.1
  388.7 5.1 multiply_convert_fusion.1
  393.9 4.5 copy.40
  398.4 5.2 reshape.163
  403.6 4.0 copy.41
  407.6 5.2 reshape.164
  412.8 6.7 %copy.49 = bf16[8,2,448,896]{3,2,0,1:T(8,128)(2,1)S(1)} copy(bf16[8,2,448,896]{3,2,1,0:T(8,128)(2,1)} %all-to-all-done) | data formatting | bytes 25690112 | tf_op jit(solution)/shard_map/all_to_all | solution.py:83
  419.6 3.4 fusion.60
  423.0 4.2 fusion.62
  427.1 13.4 %convolution_convert_fusion.1 = bf16[384,3584]{1,0:T(8,128)(2,1)} fusion(bf16[896,3584]{1,0:T(8,128)(2,1)} %param.16, bf16[384,3584]{0,1:T(8,128)(2,1)} %reshape.164, bf16[3584,896]{1,0:T(8,128)(2,1)} %bitcast.116, f32[384,896]{1,0:T(8,128)} %fusion.62), kind=kOutput, calls=%fused_computation.16 | convolution fusion | flops 4937318400 | bytes 19726336 | tf_op jit(solution)/shard_map/dot_general | solution.py:95
  440.5 128.3 %all-reduce.5.cloned.1.call-done = bf16[384,3584]{1,0:T(8,128)(2,1)} async-done(((bf16[384,3584]{1,0:T(8,128)(2,1)}), bf16[384,3584]{1,0:T(8,128)(2,1)}) %all-reduce.5.cloned.1.call-update) | async-done | bytes 2752528 | tf_op jit(solution)/shard_map/psum | solution.py:76
  568.8 2.5 fusion.11
  571.4 4.8 multiply_reduce_fusion
  576.2 8.0 %fusion.28 = bf16[384,1024]{1,0:T(8,128)(2,1)} fusion(bf16[3584,1024]{1,0:T(8,128)(2,1)} %param.17, f32[3584]{0:T(1024)S(1)} %copy-done.9, f32[384]{0:T(512)S(1)} %add_rsqrt_fusion, bf16[384,3584]{1,0:T(8,128)(2,1)S(1)} %copy-done.4, bf16[384,3584]{1,0:T(8,128)(2,1)S(1)} %copy-done, bf16[384,3584]{1,0:T(8,128)(2,1)S(1)} %copy-done.1, ...), kind=kOutput, calls=%fused_computation.51 | convolution fusion | flops 2835480576 | bytes 16431616 | tf_op jit(solution)/shard_map/dot_general | solution.py:98
  (29 shorter events, 0.1 us)
Async XLA Ops:
  6.5 79.8 %all-gather.8.cloned.1.call-start = ((), (), s32[]{:S(2)}) async-start(), calls=%async_computation.4 | async-start | bytes 13647872 | tf_op jit(solution)/shard_map/all_gather | solution.py:81
  9.4 124.9 %all-gather.4.cloned.1.call-start = ((), (), s32[]{:S(2)}) async-start(), calls=%async_computation.1 | async-start | bytes 3342336 | tf_op jit(solution)/shard_map/all_gather | solution.py:43
  11.3 157.7 %all-gather.6.cloned.1.call-start = ((), (), s32[]{:S(2)}) async-start(), calls=%async_computation.2 | async-start | bytes 3342336 | tf_op jit(solution)/shard_map/all_gather | solution.py:44
  113.6 299.2 %all-to-all-start = ((bf16[8,2,448,896]{3,2,1,0:T(8,128)(2,1)}), bf16[8,2,448,896]{3,2,1,0:T(8,128)(2,1)}, u32[]{:S(2)}, u32[]{:S(2)}) async-start(bf16[8,2,448,896]{3,2,1,0:T(8,128)(2,1)} %copy.42), calls=%async_computation | async-start | bytes 25690112 | tf_op jit(solution)/shard_map/all_to_all | solution.py:83
  119.9 262.2 %all-reduce.3.cloned.1.call-start = ((), (), s32[]{:S(2)}) async-start(), calls=%async_computation.3 | async-start | bytes 5505024 | tf_op jit(solution)/shard_map/psum | solution.py:76
  139.8 6.5 %copy-start.3 = (f32[6144,384,2]{1,0,2:T(8,128)}, f32[6144,384,2]{1,0,2:T(8,128)S(1)}, u32[]{:S(2)}) copy-start(f32[6144,384,2]{1,0,2:T(8,128)S(1)} %get-tuple-element.10) | copy-start | bytes 56623108
  169.0 13.2 %copy-start.5 = (bf16[512,3584]{1,0:T(8,128)(2,1)S(1)}, bf16[512,3584]{1,0:T(8,128)(2,1)}, u32[]{:S(2)}) copy-start(bf16[512,3584]{1,0:T(8,128)(2,1)} %param.14) | copy-start | bytes 11010052
  182.2 202.5 %copy-start.6 = (f32[3584]{0:T(1024)S(1)}, f32[3584]{0:T(1024)}, u32[]{:S(2)}) copy-start(f32[3584]{0:T(1024)} %param.18) | copy-start | bytes 43012
  185.4 203.3 %copy-start.7 = (f32[3584]{0:T(1024)S(1)}, f32[3584]{0:T(1024)}, u32[]{:S(2)}) copy-start(f32[3584]{0:T(1024)} %param.19) | copy-start | bytes 43012
  185.4 383.4 %all-reduce.5.cloned.1.call-start = ((), (), s32[]{:S(2)}) async-start(), calls=%async_computation.5 | async-start | bytes 5505024 | tf_op jit(solution)/shard_map/psum | solution.py:76
  382.1 6.6 %copy-start = (bf16[384,3584]{1,0:T(8,128)(2,1)S(1)}, bf16[384,3584]{1,0:T(8,128)(2,1)}, u32[]{:S(2)}) copy-start(bf16[384,3584]{1,0:T(8,128)(2,1)} %all-reduce.3.cloned.1.call-done) | copy-start | bytes 8257540
  419.5 3.4 copy-start.2
  440.5 130.9 %copy-start.8 = (f32[3584]{0:T(1024)S(1)}, f32[3584]{0:T(1024)}, u32[]{:S(2)}) copy-start(f32[3584]{0:T(1024)} %param.20) | copy-start | bytes 43012
  440.5 135.6 %copy-start.9 = (f32[3584]{0:T(1024)S(1)}, f32[3584]{0:T(1024)}, u32[]{:S(2)}) copy-start(f32[3584]{0:T(1024)} %param.21) | copy-start | bytes 43012
  568.8 7.4 %copy-start.1 = (bf16[384,3584]{1,0:T(8,128)(2,1)S(1)}, bf16[384,3584]{1,0:T(8,128)(2,1)}, u32[]{:S(2)}) copy-start(bf16[384,3584]{1,0:T(8,128)(2,1)} %param.11) | copy-start | bytes 8257540
  568.8 7.4 %copy-start.4 = (bf16[384,3584]{1,0:T(8,128)(2,1)S(1)}, bf16[384,3584]{1,0:T(8,128)(2,1)}, u32[]{:S(2)}) copy-start(bf16[384,3584]{1,0:T(8,128)(2,1)} %all-reduce.5.cloned.1.call-done) | copy-start | bytes 8257540
Sparse Core Ops, SparseCore 0:
  9.6 76.7 all-gather.7
  88.1 38.4 all-gather.3
  128.3 40.6 all-gather.5
  185.5 196.5 all-reduce.2
  440.6 128.1 all-reduce.4
